TPU v7x, 32 devices: a whole 2x2x4 slice. The times are simulated.
32 devices in a mesh: blk: 8 (over z, x), uly: 4 (over y, core).
Axes of the slice: x: 2, y: 2, z: 4, core: 2. Of those that a mesh axis runs over, the one named last changes fastest.
Arguments:
- query_projection: bfloat16 [4096, 4096], P(('blk', 'uly')), may hold values from -4.5 to 4.5
- key_projection: bfloat16 [4096, 512], P(('blk', 'uly')), may hold values from -4.5 to 4.5
- value_projection: bfloat16 [4096, 512], P(('blk', 'uly')), may hold values from -6 to 6
- doc_start: int32 [4096], P('blk'), may hold values from 0 to 4095, as said below
Outputs:
- attn: bfloat16 [4096, 4096], P(('blk', 'uly'))
Inputs may be any that keep to these rules, and one draw needn't show every extreme that they name: Documents are contiguous runs of positions: doc_start[0] = 0, doc_start never falls, doc_start[i] <= i, and doc_start[doc_start[i]] = doc_start[i]. Every document has at most 1024 positions; the first has exactly 1024, and another of exactly 1024 begins strictly inside a block of 512 positions. The last position begins a document of its own.
All inputs are finite; a program needn't handle non-finite values.
Results may differ from a plain program's by a relative error of at most 0.0031.
Values may be sent and summed in bfloat16 or wider, within the bound.
A program may use at most 64 MiB of HBM per device.

v0:
```python
import jax
import jax.numpy as jnp
from jax import lax
from jax.sharding import PartitionSpec as P

HEAD_WIDTH = 128
CYCLE_STEPS = 2
POSITION_GROUP = 512
masked_score = -1e30


def from_behind(block, axis, distance):
    devices = range(lax.axis_size(axis))
    route = [(i - distance, i) for i in devices if i - distance in devices]
    return lax.ppermute(block, axis, route)


def local(query_projection, key_projection, value_projection, doc_start):
    width = lax.axis_size("uly")
    tokens_dev = query_projection.shape[0]
    kv_heads = key_projection.shape[1] // HEAD_WIDTH
    repeats = max(1, width // kv_heads)

    def widen_heads(source):
        split_heads = source.reshape(tokens_dev, kv_heads, 1, HEAD_WIDTH)
        copies = jnp.broadcast_to(split_heads, (tokens_dev, kv_heads, repeats, HEAD_WIDTH))
        return copies.reshape(tokens_dev, kv_heads * repeats * HEAD_WIDTH)

    query_rows = lax.all_to_all(query_projection, "uly", split_axis=1, concat_axis=0, tiled=True)
    key_rows, value_rows = (
        lax.all_to_all(widen_heads(key_projection), "uly", split_axis=1, concat_axis=0, tiled=True),
        lax.all_to_all(
            widen_heads(value_projection), "uly", split_axis=1, concat_axis=0, tiled=True
        ),
    )
    row_count = query_rows.shape[0]
    local_kv = key_rows.shape[1] // HEAD_WIDTH
    local_q = query_rows.shape[1] // HEAD_WIDTH
    query_group_width = local_q // local_kv
    earlier = []
    for step in range(CYCLE_STEPS):
        earlier.insert(0, from_behind((key_rows, value_rows), "blk", step + 1))
    joined_keys = jnp.concatenate([piece[0] for piece in earlier] + [key_rows], axis=0).reshape(
        -1, local_kv, HEAD_WIDTH
    )
    joined_values = jnp.concatenate([piece[1] for piece in earlier] + [value_rows], axis=0).reshape(
        -1, local_kv, HEAD_WIDTH
    )
    lead = CYCLE_STEPS * row_count
    base = lax.axis_index("blk") * row_count
    anchor = base - lead
    query_heads = query_rows.reshape(row_count, local_kv, query_group_width, HEAD_WIDTH)
    score_scale = HEAD_WIDTH ** (-0.5)

    def one_tile(index):
        start = index * POSITION_GROUP
        query_tile = lax.dynamic_slice_in_dim(query_heads, start, POSITION_GROUP, 0)
        starts = lax.dynamic_slice_in_dim(doc_start, start, POSITION_GROUP, 0)
        query_places = base + start + jnp.arange(POSITION_GROUP, dtype=jnp.int32)
        first_tile = (jnp.min(starts) - anchor) // POSITION_GROUP
        last_tile = (lead + start) // POSITION_GROUP

        def add_tile(tile, carry):
            running_maximum, running_sum, running_output = carry
            key_start = tile * POSITION_GROUP
            key_tile = lax.dynamic_slice_in_dim(joined_keys, key_start, POSITION_GROUP, 0)
            value_tile = lax.dynamic_slice_in_dim(joined_values, key_start, POSITION_GROUP, 0)
            key_places = anchor + key_start + jnp.arange(POSITION_GROUP, dtype=jnp.int32)
            seen = (key_places[None, :] >= starts[:, None]) & (
                key_places[None, :] <= query_places[:, None]
            )
            seen = seen[:, None, None, :]
            scores = (
                jnp.einsum(
                    "tkgd,nkd->tkgn", query_tile, key_tile, preferred_element_type=jnp.float32
                )
                * score_scale
            )
            masked = jnp.where(seen, scores, masked_score)
            fresh = jnp.maximum(running_maximum, jnp.max(masked, axis=-1))
            factor = jnp.exp(running_maximum - fresh)
            exps = jnp.where(seen, jnp.exp(masked - fresh[..., None]), 0.0)
            running_sum = running_sum * factor + jnp.sum(exps, axis=-1)
            blended = jnp.einsum(
                "tkgn,nkd->tkgd",
                exps.astype(jnp.bfloat16),
                value_tile,
                preferred_element_type=jnp.float32,
            )
            running_output = running_output * factor[..., None] + blended
            return (fresh, running_sum, running_output)

        running_maximum = jnp.full(
            (POSITION_GROUP, local_kv, query_group_width), masked_score, jnp.float32
        )
        running_sum = jnp.zeros((POSITION_GROUP, local_kv, query_group_width), jnp.float32)
        running_output = jnp.zeros(
            (POSITION_GROUP, local_kv, query_group_width, HEAD_WIDTH), jnp.float32
        )
        running_maximum, running_sum, running_output = lax.fori_loop(
            first_tile, last_tile + 1, add_tile, (running_maximum, running_sum, running_output)
        )
        return (running_output / running_sum[..., None]).astype(jnp.bfloat16)

    outputs = lax.map(one_tile, jnp.arange(row_count // POSITION_GROUP, dtype=jnp.int32))
    attn = outputs.reshape(row_count, local_q * HEAD_WIDTH)
    return lax.all_to_all(attn, "uly", split_axis=0, concat_axis=1, tiled=True)


def solution(mesh):
    placed = (P(("blk", "uly"), None), P(("blk", "uly"), None), P(("blk", "uly"), None), P("blk"))
    return jax.shard_map(
        local, mesh=mesh, in_specs=placed, out_specs=P(("blk", "uly"), None), check_vma=False
    )
```

profile of v0, /device:TPU:18, one launch (start us, length us, event | category | flops | bytes accessed | tf_op | source)
XLA Modules:
  0.0 90.7 jit_solution(1253593889368224903)
XLA Ops:
  0.0 1.7 %copy.24 = bf16[128,512]{0,1:T(8,128)(2,1)} copy(bf16[128,512]{1,0:T(8,128)(2,1)} %param.8) | data formatting | bytes 262144 | tf_op args[2]
  1.7 3.3 %all-to-all-start.2 = ((bf16[128,4,128]{0,2,1:T(8,128)(2,1)}), bf16[128,4,128]{0,2,1:T(8,128)(2,1)S(1)}, u32[]{:S(2)}, u32[]{:S(2)}) async-start(bf16[128,4,128]{0,2,1:T(8,128)(2,1)} %bitcast.5), calls=%async_computation.2 | async-start | bytes 262144 | tf_op jit(solution)/shard_map/all_to_all | solution.py:32
  5.7 3.9 %all-to-all-done.2 = bf16[128,4,128]{0,2,1:T(8,128)(2,1)S(1)} async-done(((bf16[128,4,128]{0,2,1:T(8,128)(2,1)}), bf16[128,4,128]{0,2,1:T(8,128)(2,1)S(1)}, u32[]{:S(2)}, u32[]{:S(2)}) %all-to-all-start.2) | async-done | bytes 131104 | tf_op jit(solution)/shard_map/all_to_all | solution.py:32
  9.6 3.3 %all-to-all-start = ((bf16[128,4,128]{2,0,1:T(8,128)(2,1)}), bf16[128,4,128]{2,0,1:T(8,128)(2,1)S(1)}, u32[]{:S(2)}, u32[]{:S(2)}) async-start(bf16[128,4,128]{2,0,1:T(8,128)(2,1)} %copy_bitcast_fusion.1), calls=%async_computation | async-start | bytes 262144 | tf_op jit(solution)/shard_map/all_to_all | solution.py:31
  12.9 2.3 %copy.39 = bf16[16,4,8,1024]{3,2,0,1:T(8,128)(2,1)} copy(bf16[16,4,8,1024]{3,2,1,0:T(8,128)(2,1)} %bitcast.111) | data formatting | bytes 2097152 | tf_op jit(solution)/shard_map/all_to_all | solution.py:29
  15.2 2.3 %all-to-all-done = bf16[128,4,128]{2,0,1:T(8,128)(2,1)S(1)} async-done(((bf16[128,4,128]{2,0,1:T(8,128)(2,1)}), bf16[128,4,128]{2,0,1:T(8,128)(2,1)S(1)}, u32[]{:S(2)}, u32[]{:S(2)}) %all-to-all-start) | async-done | bytes 131104 | tf_op jit(solution)/shard_map/all_to_all | solution.py:31
  17.5 3.5 %all-to-all-start.1 = ((bf16[128,4,1024]{2,0,1:T(8,128)(2,1)}), bf16[128,4,1024]{2,0,1:T(8,128)(2,1)S(1)}, u32[]{:S(2)}, u32[]{:S(2)}) async-start(bf16[128,4,1024]{2,0,1:T(8,128)(2,1)} %bitcast.83), calls=%async_computation.1 | async-start | bytes 2097152 | tf_op jit(solution)/shard_map/all_to_all | solution.py:29
  21.2 3.5 %collective-permute-start.2 = (bf16[512,128]{1,0:T(8,128)(2,1)S(1)}, bf16[512,128]{1,0:T(8,128)(2,1)S(1)}, u32[]{:S(2)}, u32[]{:S(2)}) collective-permute-start(bf16[512,128]{1,0:T(8,128)(2,1)S(1)} %bitcast.116), channel_id=1, source_target_pairs={{0,8},{4,12},{8,16},{12,20},{16,24},{20,28},{1,9},{5,13},{9,17},{1... | collective-permute-start | bytes 393224 | tf_op jit(solution)/shard_map/ppermute | solution.py:15
  24.7 1.9 %collective-permute-start.3 = (bf16[512,128]{1,0:T(8,128)(2,1)S(1)}, bf16[512,128]{1,0:T(8,128)(2,1)S(1)}, u32[]{:S(2)}, u32[]{:S(2)}) collective-permute-start(bf16[512,128]{1,0:T(8,128)(2,1)S(1)} %bitcast.117), channel_id=1, source_target_pairs={{0,4},{4,8},{8,12},{12,16},{16,20},{20,24},{24,28},{1,5},{5,9},{9,... | collective-permute-start | bytes 393224 | tf_op jit(solution)/shard_map/ppermute | solution.py:15
  26.6 1.4 %reduce_min.10 = s32[]{:T(128)} reduce(s32[512]{0:T(512)} %param.9, s32[]{:T(128)} %constant.93.clone.1), dimensions={0}, to_apply=%region_0.1 | reduce | flops 511 | bytes 2056 | tf_op jit(solution)/shard_map/while/body/eval_jaxpr/reduce_min | solution.py:60
  28.7 1.9 %collective-permute-start = (bf16[512,128]{1,0:T(8,128)(2,1)S(1)}, bf16[512,128]{1,0:T(8,128)(2,1)S(1)}, u32[]{:S(2)}, u32[]{:S(2)}) collective-permute-start(bf16[512,128]{1,0:T(8,128)(2,1)S(1)} %bitcast.113), channel_id=1, source_target_pairs={{0,8},{4,12},{8,16},{12,20},{16,24},{20,28},{1,9},{5,13},{9,17},{1... | collective-permute-start | bytes 393224 | tf_op jit(solution)/shard_map/ppermute | solution.py:15
  30.6 2.1 %collective-permute-start.1 = (bf16[512,128]{1,0:T(8,128)(2,1)S(1)}, bf16[512,128]{1,0:T(8,128)(2,1)S(1)}, u32[]{:S(2)}, u32[]{:S(2)}) collective-permute-start(bf16[512,128]{1,0:T(8,128)(2,1)S(1)} %bitcast.114), channel_id=1, source_target_pairs={{0,4},{4,8},{8,12},{12,16},{16,20},{20,24},{24,28},{1,5},{5,9},{9,... | collective-permute-start | bytes 393224 | tf_op jit(solution)/shard_map/ppermute | solution.py:15
  32.8 0.8 maximum_bitcast_fusion.1
  33.5 2.6 %collective-permute-done = bf16[512,128]{1,0:T(8,128)(2,1)S(1)} collective-permute-done((bf16[512,128]{1,0:T(8,128)(2,1)S(1)}, bf16[512,128]{1,0:T(8,128)(2,1)S(1)}, u32[]{:S(2)}, u32[]{:S(2)}) %collective-permute-start) | collective-permute-done | bytes 131104 | tf_op jit(solution)/shard_map/ppermute | solution.py:15
  36.2 1.9 %collective-permute-done.1 = bf16[512,128]{1,0:T(8,128)(2,1)S(1)} collective-permute-done((bf16[512,128]{1,0:T(8,128)(2,1)S(1)}, bf16[512,128]{1,0:T(8,128)(2,1)S(1)}, u32[]{:S(2)}, u32[]{:S(2)}) %collective-permute-start.1) | collective-permute-done | bytes 131104 | tf_op jit(solution)/shard_map/ppermute | solution.py:15
  38.1 0.8 maximum_bitcast_fusion
  40.2 29.5 %while.24 = (s32[]{:T(128)}, f32[512,1,8]{0,2,1:T(8,128)S(1)}, f32[512,1,8]{0,2,1:T(8,128)}, f32[512,1,8,128]{0,3,2,1:T(8,128)S(1)}, s32[]{:T(128)}, /*index=5*/...) while((s32[]{:T(128)}, f32[512,1,8]{0,2,1:T(8,128)S(1)}, ...), condition=%wide.region_4.5_spmd.clone, body=%wide.region_1.4_spmd.clone.sunk | while | flops 1102853120 | bytes 32123144 | solution.py:100
  40.2 0.9 %compare_and_fusion.2 = pred[512,512]{0,1:T(8,128)(4,1)S(1)} fusion(s32[512]{0:T(512)S(1)} %get-tuple-element.256, s32[512]{0:T(512)} %get-tuple-element.295, s32[512]{0:T(512)S(1)} %get-tuple-element.257), kind=kLoop, calls=%fused_computation.12.clone.1 | loop fusion | flops 786432 | bytes 268288 | tf_op jit(solution)/shard_map/while/body/eval_jaxpr/while/body/and | solution.py:69
  41.1 2.4 %fusion.31 = (f32[512,8]{0,1:T(8,128)S(1)}, f32[512,512,8]{1,0,2:T(8,128)S(1)}) fusion(pred[512,512]{0,1:T(8,128)(4,1)S(1)} %compare_and_fusion.2, bf16[512,1,8,128]{3,0,2,1:T(8,128)(2,1)S(1)} %get-tuple-element.297, bf16[1536,1,128]{2,0,1:T(8,128)(2,1)} %get-tuple-element.296, s32[]{:T(128)S(6)} %select_n.64), kind=kOutput, calls=%fused_computation.3.clone.1 | convolution fusion | flops 543158272 | bytes 9846788 | tf_op jit(solution)/shard_map/while/body/eval_jaxpr/while/body/tkgd,nkd->tkgn/dot_general | solution.py:74
  43.6 3.7 %bitcast_add_fusion.5 = f32[512,1,8,128]{0,3,2,1:T(8,128)S(1)} fusion(f32[512,1,8,128]{0,3,2,1:T(8,128)S(1)} %get-tuple-element.279, f32[512,512,8]{1,0,2:T(8,128)S(1)} %get-tuple-element.260, f32[512,8]{0,1:T(8,128)S(1)} %bitcast.106, pred[512,512]{0,1:T(8,128)(4,1)S(1)} %compare_and_fusion.2, f32[512,8]{0,1:T(8,128)S(1)} %get-tuple-element.261, ...), kind=kOutput, calls=%fused_computation.9.clone.1 | convolution fusion | flops 548405248 | bytes 13008900 | tf_op jit(solution)/shard_map/while/body/eval_jaxpr/while/body/tkgn,nkd->tkgd/dot_general | solution.py:84
  47.3 2.0 %fusion.33 = f32[512,8]{0,1:T(8,128)S(1)} fusion(f32[512,512,8]{1,0,2:T(8,128)S(1)} %get-tuple-element.260, f32[512,8]{0,1:T(8,128)S(1)} %bitcast.107, pred[512,512]{0,1:T(8,128)(4,1)S(1)} %compare_and_fusion.2), kind=kLoop, calls=%fused_computation.5.clone.1 | loop fusion | flops 10481664 | bytes 8683520 | tf_op jit(solution)/shard_map/while/body/eval_jaxpr/while/body/reduce_sum | solution.py:83
  50.0 0.9 %compare_and_fusion.2 = pred[512,512]{0,1:T(8,128)(4,1)S(1)} fusion(s32[512]{0:T(512)S(1)} %get-tuple-element.256, s32[512]{0:T(512)} %get-tuple-element.295, s32[512]{0:T(512)S(1)} %get-tuple-element.257), kind=kLoop, calls=%fused_computation.12.clone.1 | loop fusion | flops 786432 | bytes 268288 | tf_op jit(solution)/shard_map/while/body/eval_jaxpr/while/body/and | solution.py:69
  51.0 2.4 %fusion.31 = (f32[512,8]{0,1:T(8,128)S(1)}, f32[512,512,8]{1,0,2:T(8,128)S(1)}) fusion(pred[512,512]{0,1:T(8,128)(4,1)S(1)} %compare_and_fusion.2, bf16[512,1,8,128]{3,0,2,1:T(8,128)(2,1)S(1)} %get-tuple-element.297, bf16[1536,1,128]{2,0,1:T(8,128)(2,1)} %get-tuple-element.296, s32[]{:T(128)S(6)} %select_n.64), kind=kOutput, calls=%fused_computation.3.clone.1 | convolution fusion | flops 543158272 | bytes 9846788 | tf_op jit(solution)/shard_map/while/body/eval_jaxpr/while/body/tkgd,nkd->tkgn/dot_general | solution.py:74
  53.4 3.7 %bitcast_add_fusion.5 = f32[512,1,8,128]{0,3,2,1:T(8,128)S(1)} fusion(f32[512,1,8,128]{0,3,2,1:T(8,128)S(1)} %get-tuple-element.279, f32[512,512,8]{1,0,2:T(8,128)S(1)} %get-tuple-element.260, f32[512,8]{0,1:T(8,128)S(1)} %bitcast.106, pred[512,512]{0,1:T(8,128)(4,1)S(1)} %compare_and_fusion.2, f32[512,8]{0,1:T(8,128)S(1)} %get-tuple-element.261, ...), kind=kOutput, calls=%fused_computation.9.clone.1 | convolution fusion | flops 548405248 | bytes 13008900 | tf_op jit(solution)/shard_map/while/body/eval_jaxpr/while/body/tkgn,nkd->tkgd/dot_general | solution.py:84
  57.1 2.0 %fusion.33 = f32[512,8]{0,1:T(8,128)S(1)} fusion(f32[512,512,8]{1,0,2:T(8,128)S(1)} %get-tuple-element.260, f32[512,8]{0,1:T(8,128)S(1)} %bitcast.107, pred[512,512]{0,1:T(8,128)(4,1)S(1)} %compare_and_fusion.2), kind=kLoop, calls=%fused_computation.5.clone.1 | loop fusion | flops 10481664 | bytes 8683520 | tf_op jit(solution)/shard_map/while/body/eval_jaxpr/while/body/reduce_sum | solution.py:83
  59.8 0.9 %compare_and_fusion.2 = pred[512,512]{0,1:T(8,128)(4,1)S(1)} fusion(s32[512]{0:T(512)S(1)} %get-tuple-element.256, s32[512]{0:T(512)} %get-tuple-element.295, s32[512]{0:T(512)S(1)} %get-tuple-element.257), kind=kLoop, calls=%fused_computation.12.clone.1 | loop fusion | flops 786432 | bytes 268288 | tf_op jit(solution)/shard_map/while/body/eval_jaxpr/while/body/and | solution.py:69
  60.8 2.4 %fusion.31 = (f32[512,8]{0,1:T(8,128)S(1)}, f32[512,512,8]{1,0,2:T(8,128)S(1)}) fusion(pred[512,512]{0,1:T(8,128)(4,1)S(1)} %compare_and_fusion.2, bf16[512,1,8,128]{3,0,2,1:T(8,128)(2,1)S(1)} %get-tuple-element.297, bf16[1536,1,128]{2,0,1:T(8,128)(2,1)} %get-tuple-element.296, s32[]{:T(128)S(6)} %select_n.64), kind=kOutput, calls=%fused_computation.3.clone.1 | convolution fusion | flops 543158272 | bytes 9846788 | tf_op jit(solution)/shard_map/while/body/eval_jaxpr/while/body/tkgd,nkd->tkgn/dot_general | solution.py:74
  63.2 3.7 %bitcast_add_fusion.5 = f32[512,1,8,128]{0,3,2,1:T(8,128)S(1)} fusion(f32[512,1,8,128]{0,3,2,1:T(8,128)S(1)} %get-tuple-element.279, f32[512,512,8]{1,0,2:T(8,128)S(1)} %get-tuple-element.260, f32[512,8]{0,1:T(8,128)S(1)} %bitcast.106, pred[512,512]{0,1:T(8,128)(4,1)S(1)} %compare_and_fusion.2, f32[512,8]{0,1:T(8,128)S(1)} %get-tuple-element.261, ...), kind=kOutput, calls=%fused_computation.9.clone.1 | convolution fusion | flops 548405248 | bytes 13008900 | tf_op jit(solution)/shard_map/while/body/eval_jaxpr/while/body/tkgn,nkd->tkgd/dot_general | solution.py:84
  67.0 2.0 %fusion.33 = f32[512,8]{0,1:T(8,128)S(1)} fusion(f32[512,512,8]{1,0,2:T(8,128)S(1)} %get-tuple-element.260, f32[512,8]{0,1:T(8,128)S(1)} %bitcast.107, pred[512,512]{0,1:T(8,128)(4,1)S(1)} %compare_and_fusion.2), kind=kLoop, calls=%fused_computation.5.clone.1 | loop fusion | flops 10481664 | bytes 8683520 | tf_op jit(solution)/shard_map/while/body/eval_jaxpr/while/body/reduce_sum | solution.py:83
  69.7 1.0 %divide_convert_fusion = bf16[512,1,8,128]{0,3,2,1:T(8,128)(2,1)S(1)} fusion(f32[512,1,8,128]{0,3,2,1:T(8,128)S(1)} %get-tuple-element.108, f32[512,8]{0,1:T(8,128)} %bitcast.112), kind=kLoop, calls=%fused_computation.28 | loop fusion | flops 1048576 | bytes 3162112 | tf_op jit(solution)/shard_map/while/body/eval_jaxpr/convert_element_type | solution.py:103
  71.6 17.1 %all_to_all.73 = bf16[4,128,1024]{2,1,0:T(8,128)(2,1)S(1)} all-to-all(bf16[4,128,1024]{2,1,0:T(8,128)(2,1)S(1)} %copy.32), channel_id=1, replica_groups=mesh['blk'=8,'uly'=4] {'uly'}, dimensions={0} | all-to-all | bytes 2097152 | tf_op jit(solution)/shard_map/all_to_all | solution.py:107
  89.4 1.3 %copy.30 = bf16[128,4096]{1,0:T(8,128)(2,1)} copy(bf16[128,4096]{0,1:T(8,128)(2,1)S(1)} %bitcast.110) | data formatting | bytes 2097152 | tf_op jit(solution)/shard_map/all_to_all | solution.py:107
  (39 shorter events, 5.6 us)
Async XLA Ops:
  0.0 5.0 %copy-start = (bf16[128,512]{1,0:T(8,128)(2,1)S(1)}, bf16[128,512]{1,0:T(8,128)(2,1)}, u32[]{:S(2)}) copy-start(bf16[128,512]{1,0:T(8,128)(2,1)} %param.7) | copy-start | bytes 393220
  1.7 7.9 %all-to-all-start.2 = ((bf16[128,4,128]{0,2,1:T(8,128)(2,1)}), bf16[128,4,128]{0,2,1:T(8,128)(2,1)S(1)}, u32[]{:S(2)}, u32[]{:S(2)}) async-start(bf16[128,4,128]{0,2,1:T(8,128)(2,1)} %bitcast.5), calls=%async_computation.2 | async-start | bytes 262144 | tf_op jit(solution)/shard_map/all_to_all | solution.py:32
  9.6 7.9 %all-to-all-start = ((bf16[128,4,128]{2,0,1:T(8,128)(2,1)}), bf16[128,4,128]{2,0,1:T(8,128)(2,1)S(1)}, u32[]{:S(2)}, u32[]{:S(2)}) async-start(bf16[128,4,128]{2,0,1:T(8,128)(2,1)} %copy_bitcast_fusion.1), calls=%async_computation | async-start | bytes 262144 | tf_op jit(solution)/shard_map/all_to_all | solution.py:31
  17.5 21.4 %all-to-all-start.1 = ((bf16[128,4,1024]{2,0,1:T(8,128)(2,1)}), bf16[128,4,1024]{2,0,1:T(8,128)(2,1)S(1)}, u32[]{:S(2)}, u32[]{:S(2)}) async-start(bf16[128,4,1024]{2,0,1:T(8,128)(2,1)} %bitcast.83), calls=%async_computation.1 | async-start | bytes 2097152 | tf_op jit(solution)/shard_map/all_to_all | solution.py:29
  21.2 11.6 %collective-permute-start.2 = (bf16[512,128]{1,0:T(8,128)(2,1)S(1)}, bf16[512,128]{1,0:T(8,128)(2,1)S(1)}, u32[]{:S(2)}, u32[]{:S(2)}) collective-permute-start(bf16[512,128]{1,0:T(8,128)(2,1)S(1)} %bitcast.116), channel_id=1, source_target_pairs={{0,8},{4,12},{8,16},{12,20},{16,24},{20,28},{1,9},{5,13},{9,17},{1... | collective-permute-start | bytes 393224 | tf_op jit(solution)/shard_map/ppermute | solution.py:15
  24.7 8.1 %collective-permute-start.3 = (bf16[512,128]{1,0:T(8,128)(2,1)S(1)}, bf16[512,128]{1,0:T(8,128)(2,1)S(1)}, u32[]{:S(2)}, u32[]{:S(2)}) collective-permute-start(bf16[512,128]{1,0:T(8,128)(2,1)S(1)} %bitcast.117), channel_id=1, source_target_pairs={{0,4},{4,8},{8,12},{12,16},{16,20},{20,24},{24,28},{1,5},{5,9},{9,... | collective-permute-start | bytes 393224 | tf_op jit(solution)/shard_map/ppermute | solution.py:15
  28.7 7.5 %collective-permute-start = (bf16[512,128]{1,0:T(8,128)(2,1)S(1)}, bf16[512,128]{1,0:T(8,128)(2,1)S(1)}, u32[]{:S(2)}, u32[]{:S(2)}) collective-permute-start(bf16[512,128]{1,0:T(8,128)(2,1)S(1)} %bitcast.113), channel_id=1, source_target_pairs={{0,8},{4,12},{8,16},{12,20},{16,24},{20,28},{1,9},{5,13},{9,17},{1... | collective-permute-start | bytes 393224 | tf_op jit(solution)/shard_map/ppermute | solution.py:15
  30.6 7.5 %collective-permute-start.1 = (bf16[512,128]{1,0:T(8,128)(2,1)S(1)}, bf16[512,128]{1,0:T(8,128)(2,1)S(1)}, u32[]{:S(2)}, u32[]{:S(2)}) collective-permute-start(bf16[512,128]{1,0:T(8,128)(2,1)S(1)} %bitcast.114), channel_id=1, source_target_pairs={{0,4},{4,8},{8,12},{12,16},{16,20},{20,24},{24,28},{1,5},{5,9},{9,... | collective-permute-start | bytes 393224 | tf_op jit(solution)/shard_map/ppermute | solution.py:15
  43.6 5.8 %copy-start.1 = (f32[512,1,8]{0,2,1:T(8,128)S(1)}, f32[512,1,8]{0,2,1:T(8,128)}, u32[]{:S(2)}) copy-start(f32[512,1,8]{0,2,1:T(8,128)} %get-tuple-element.278) | copy-start | bytes 49156 | tf_op jit(solution)/shard_map/while/body/eval_jaxpr/while
  49.4 0.6 copy-start.2
  53.4 5.8 %copy-start.1 = (f32[512,1,8]{0,2,1:T(8,128)S(1)}, f32[512,1,8]{0,2,1:T(8,128)}, u32[]{:S(2)}) copy-start(f32[512,1,8]{0,2,1:T(8,128)} %get-tuple-element.278) | copy-start | bytes 49156 | tf_op jit(solution)/shard_map/while/body/eval_jaxpr/while
  59.2 0.6 copy-start.2
  63.2 5.8 %copy-start.1 = (f32[512,1,8]{0,2,1:T(8,128)S(1)}, f32[512,1,8]{0,2,1:T(8,128)}, u32[]{:S(2)}) copy-start(f32[512,1,8]{0,2,1:T(8,128)} %get-tuple-element.278) | copy-start | bytes 49156 | tf_op jit(solution)/shard_map/while/body/eval_jaxpr/while
  69.0 0.6 copy-start.2
where the time goes:
time: 91.6 us; the launch traced here: 90.7 us
  starting transfers between devices  19.6 us (21%)
  matrix products  18.4 us (20%)
  blocking collectives  17.1 us (19%)
  other arithmetic  13 us (14%)
  local copies, waits for them, and re-layouts  10.8 us (12%)
  waiting for transfers between devices  10.7 us (12%)
    all_to_all x1, blocking collectives, local(): return lax.all_to_all(attn, 'uly', split_axis=0, concat_axis=1, tiled=True)  17.1 us
    dot_general x3, matrix products, add_tile(): jnp.einsum('tkgn,nkd->tkgd', exps.astype(jnp.bfloat16), value_tile, prefe...  11.2 us
    ppermute x4, starting transfers between devices, from_behind(): return lax.ppermute(block, axis, route)  9.44 us
    dot_general x3, matrix products, add_tile(): jnp.einsum('tkgd,nkd->tkgn', query_tile, key_tile, preferred_element_type...  7.21 us
    reduce_sum x3, other arithmetic, add_tile(): running_sum = running_sum * factor + jnp.sum(exps, axis=-1)  6.1 us
    ppermute x4, waiting for transfers between devices, from_behind(): return lax.ppermute(block, axis, route)  4.56 us
    all_to_all x1, waiting for transfers between devices, local(): lax.all_to_all(widen_heads(value_projection), 'uly', split_axis=1, concat...  3.88 us
    all_to_all x1, starting transfers between devices, local(): lax.all_to_all(query_projection, 'uly', split_axis=1, concat_axis=0, tile...  3.52 us
  transfers between devices with their start and end apart: 7, of which 4 were waited for; matrix products, arithmetic and copies ran while one was open for 7% of the time, Pallas kernels for 0%

commit v1 on v0

--- a/solution.py
+++ b/solution.py
@@ -7,6 +7,32 @@
 CYCLE_STEPS = 2
 POSITION_GROUP = 512
 masked_score = -1e30
+
+
+def solve_the_flows(arr_in, dim_at, field_in):
+    top, local_out = (arr_in.shape[:dim_at], arr_in.shape[dim_at + 1 :])
+    return jnp.moveaxis(arr_in.reshape(*top, field_in, -1, *local_out), dim_at, 0)
+
+
+def _link_group(page, d0):
+    page = jnp.moveaxis(page, 0, d0)
+    r2 = page.shape
+    return page.reshape(*r2[:d0], r2[d0] * r2[d0 + 1], *r2[d0 + 2 :])
+
+
+def lay_sample(xin, mesh_ax, sheet, view):
+    response, field_out = (lax.axis_size(mesh_ax), lax.axis_index(mesh_ax))
+    left_arr = solve_the_flows(xin, sheet, response)
+    f_now = left_arr
+    for d in range(1, response):
+        q_next, state_now = ((field_out + d) % response, (field_out - d) % response)
+        big = lax.dynamic_index_in_dim(left_arr, q_next, 0)
+        history = []
+        for hop_no in range(response):
+            history.append((hop_no, (hop_no + d) % response))
+        wide_out = lax.ppermute(big, axis_name=mesh_ax, perm=history)
+        f_now = lax.dynamic_update_slice_in_dim(f_now, wide_out, state_now, axis=0)
+    return _link_group(f_now, view)
 
 
 def from_behind(block, axis, distance):
@@ -28,7 +54,7 @@
 
     query_rows = lax.all_to_all(query_projection, "uly", split_axis=1, concat_axis=0, tiled=True)
     key_rows, value_rows = (
-        lax.all_to_all(widen_heads(key_projection), "uly", split_axis=1, concat_axis=0, tiled=True),
+        lay_sample(widen_heads(key_projection), "uly", 1, 0),
         lax.all_to_all(
             widen_heads(value_projection), "uly", split_axis=1, concat_axis=0, tiled=True
         ),

time: 91.6 us -> 82.6 us (0.902)
  waiting for transfers between devices: 10.7 us -> 6.78 us
  other arithmetic: 13 us -> 10.2 us
  local copies, waits for them, and re-layouts: 10.8 us -> 8.89 us
    all_to_all x1 -> x0, starting transfers between devices: 3.32 us -> none  [local(): lax.all_to_all(widen_heads(key_projection), 'uly', split_axis=1, concat_a...]
    ppermute x0 -> x3, starting transfers between devices: none -> 3.03 us  [lay_sample(): wide_out = lax.ppermute(big, axis_name=mesh_ax, perm=history)]
    all_to_all x1 -> x0, waiting for transfers between devices: 2.28 us -> none  [local(): lax.all_to_all(widen_heads(key_projection), 'uly', split_axis=1, concat_a...]
    and x3, other arithmetic: 2.85 us -> 0.81 us  [add_tile(): (key_places[None, :] >= starts[:, None]) & (key_places[None, :] <= query_...]
    while x15 -> x3, local copies, waits for them, and re-layouts: 1.83 us -> 0.01 us
    all_to_all x1, waiting for transfers between devices: 3.88 us -> 2.21 us  [local(): lax.all_to_all(widen_heads(value_projection), 'uly', split_axis=1, concat...]
    unnamed x5 -> x6, local copies, waits for them, and re-layouts: 2.11 us -> 3.1 us
  transfers between devices with their start and end apart: 7 -> 9, of which waited for: 4 -> 3; matrix products, arithmetic and copies ran while one was open for 7% -> 9% of each run, Pallas kernels for 0% -> 0%
where the time goes in v1:
time: 82.6 us; the launch traced here: 82 us
  starting transfers between devices  19.3 us (23%)
  matrix products  18.4 us (22%)
  blocking collectives  17.1 us (21%)
  other arithmetic  10.2 us (12%)
  local copies, waits for them, and re-layouts  8.89 us (11%)
  waiting for transfers between devices  6.78 us (8%)
  between operations  1.01 us (1%)
    all_to_all x1, blocking collectives, local(): return lax.all_to_all(attn, 'uly', split_axis=0, concat_axis=1, tiled=True)  17.1 us
    dot_general x3, matrix products, add_tile(): jnp.einsum('tkgn,nkd->tkgd', exps.astype(jnp.bfloat16), value_tile, prefe...  11.2 us
    ppermute x4, starting transfers between devices, from_behind(): return lax.ppermute(block, axis, route)  9.44 us
    dot_general x3, matrix products, add_tile(): jnp.einsum('tkgd,nkd->tkgn', query_tile, key_tile, preferred_element_type...  7.21 us
    reduce_sum x3, other arithmetic, add_tile(): running_sum = running_sum * factor + jnp.sum(exps, axis=-1)  6.1 us
    ppermute x4, waiting for transfers between devices, from_behind(): return lax.ppermute(block, axis, route)  4.56 us
    all_to_all x1, starting transfers between devices, local(): lax.all_to_all(query_projection, 'uly', split_axis=1, concat_axis=0, tile...  3.52 us
    all_to_all x1, starting transfers between devices, local(): lax.all_to_all(widen_heads(value_projection), 'uly', split_axis=1, concat...  3.32 us
  transfers between devices with their start and end apart: 9, of which 3 were waited for; matrix products, arithmetic and copies ran while one was open for 9% of the time, Pallas kernels for 0%

profile of v1, /device:TPU:18, one launch (start us, length us, event | category | flops | bytes accessed | tf_op | source)
XLA Modules:
  0.0 82.0 jit_solution(11042134039627610143)
XLA Ops:
  0.0 1.0 %copy.53 = bf16[128,512]{0,1:T(8,128)(2,1)S(1)} copy(bf16[128,512]{1,0:T(8,128)(2,1)} %param.7) | data formatting | bytes 262144 | tf_op args[1]
  1.1 1.6 %collective-permute-start.1 = (bf16[1,128,128]{1,2,0:T(8,128)(2,1)S(1)}, bf16[1,128,128]{1,2,0:T(8,128)(2,1)S(1)}, u32[]{:S(2)}, u32[]{:S(2)}) collective-permute-start(bf16[1,128,128]{1,2,0:T(8,128)(2,1)S(1)} %get-tuple-element.210), channel_id=1, source_target_pairs={{0,2},{1,3},{2,0},{3,1},{4,6},{5,7},{6,4},{7,5},{8,10},{9,11},{10,... | collective-permute-start | bytes 98312 | tf_op jit(solution)/shard_map/ppermute | solution.py:33
  2.7 1.4 %collective-permute-start.2 = (bf16[1,128,128]{1,2,0:T(8,128)(2,1)S(1)}, bf16[1,128,128]{1,2,0:T(8,128)(2,1)S(1)}, u32[]{:S(2)}, u32[]{:S(2)}) collective-permute-start(bf16[1,128,128]{1,2,0:T(8,128)(2,1)S(1)} %get-tuple-element.209), channel_id=1, source_target_pairs={{0,3},{1,0},{2,1},{3,2},{4,7},{5,4},{6,5},{7,6},{8,11},{9,8},{10,9... | collective-permute-start | bytes 98312 | tf_op jit(solution)/shard_map/ppermute | solution.py:33
  4.1 1.7 %copy.62 = bf16[128,512]{0,1:T(8,128)(2,1)} copy(bf16[128,512]{1,0:T(8,128)(2,1)} %param.8) | data formatting | bytes 262144 | tf_op args[2]
  5.8 3.3 %all-to-all-start.1 = ((bf16[128,4,128]{0,2,1:T(8,128)(2,1)}), bf16[128,4,128]{0,2,1:T(8,128)(2,1)S(1)}, u32[]{:S(2)}, u32[]{:S(2)}) async-start(bf16[128,4,128]{0,2,1:T(8,128)(2,1)} %bitcast.8), calls=%async_computation.1 | async-start | bytes 262144 | tf_op jit(solution)/shard_map/all_to_all | solution.py:58
  9.2 2.3 %copy.78 = bf16[16,4,8,1024]{3,2,0,1:T(8,128)(2,1)} copy(bf16[16,4,8,1024]{3,2,1,0:T(8,128)(2,1)} %bitcast.113) | data formatting | bytes 2097152 | tf_op jit(solution)/shard_map/all_to_all | solution.py:55
  11.5 2.2 %all-to-all-done.1 = bf16[128,4,128]{0,2,1:T(8,128)(2,1)S(1)} async-done(((bf16[128,4,128]{0,2,1:T(8,128)(2,1)}), bf16[128,4,128]{0,2,1:T(8,128)(2,1)S(1)}, u32[]{:S(2)}, u32[]{:S(2)}) %all-to-all-start.1) | async-done | bytes 131104 | tf_op jit(solution)/shard_map/all_to_all | solution.py:58
  13.7 3.5 %all-to-all-start = ((bf16[128,4,1024]{2,0,1:T(8,128)(2,1)}), bf16[128,4,1024]{2,0,1:T(8,128)(2,1)S(1)}, u32[]{:S(2)}, u32[]{:S(2)}) async-start(bf16[128,4,1024]{2,0,1:T(8,128)(2,1)} %bitcast.85), calls=%async_computation | async-start | bytes 2097152 | tf_op jit(solution)/shard_map/all_to_all | solution.py:55
  17.4 3.5 %collective-permute-start.3 = (bf16[512,128]{1,0:T(8,128)(2,1)S(1)}, bf16[512,128]{1,0:T(8,128)(2,1)S(1)}, u32[]{:S(2)}, u32[]{:S(2)}) collective-permute-start(bf16[512,128]{1,0:T(8,128)(2,1)S(1)} %bitcast.117), channel_id=1, source_target_pairs={{0,8},{4,12},{8,16},{12,20},{16,24},{20,28},{1,9},{5,13},{9,17},{1... | collective-permute-start | bytes 393224 | tf_op jit(solution)/shard_map/ppermute | solution.py:41
  20.9 1.9 %collective-permute-start.4 = (bf16[512,128]{1,0:T(8,128)(2,1)S(1)}, bf16[512,128]{1,0:T(8,128)(2,1)S(1)}, u32[]{:S(2)}, u32[]{:S(2)}) collective-permute-start(bf16[512,128]{1,0:T(8,128)(2,1)S(1)} %bitcast.118), channel_id=1, source_target_pairs={{0,4},{4,8},{8,12},{12,16},{16,20},{20,24},{24,28},{1,5},{5,9},{9,... | collective-permute-start | bytes 393224 | tf_op jit(solution)/shard_map/ppermute | solution.py:41
  22.8 1.4 %reduce_min.10 = s32[]{:T(128)} reduce(s32[512]{0:T(512)} %param.9, s32[]{:T(128)} %constant.139.clone.1), dimensions={0}, to_apply=%region_0.1 | reduce | flops 511 | bytes 2056 | tf_op jit(solution)/shard_map/while/body/eval_jaxpr/reduce_min | solution.py:86
  25.1 1.9 %collective-permute-start.5 = (bf16[512,128]{1,0:T(8,128)(2,1)S(1)}, bf16[512,128]{1,0:T(8,128)(2,1)S(1)}, u32[]{:S(2)}, u32[]{:S(2)}) collective-permute-start(bf16[512,128]{1,0:T(8,128)(2,1)S(1)} %bitcast.120), channel_id=1, source_target_pairs={{0,8},{4,12},{8,16},{12,20},{16,24},{20,28},{1,9},{5,13},{9,17},{1... | collective-permute-start | bytes 393224 | tf_op jit(solution)/shard_map/ppermute | solution.py:41
  27.0 2.1 %collective-permute-start.6 = (bf16[512,128]{1,0:T(8,128)(2,1)S(1)}, bf16[512,128]{1,0:T(8,128)(2,1)S(1)}, u32[]{:S(2)}, u32[]{:S(2)}) collective-permute-start(bf16[512,128]{1,0:T(8,128)(2,1)S(1)} %bitcast.121), channel_id=1, source_target_pairs={{0,4},{4,8},{8,12},{12,16},{16,20},{20,24},{24,28},{1,5},{5,9},{9,... | collective-permute-start | bytes 393224 | tf_op jit(solution)/shard_map/ppermute | solution.py:41
  29.1 0.8 maximum_bitcast_fusion
  29.9 2.6 %collective-permute-done.5 = bf16[512,128]{1,0:T(8,128)(2,1)S(1)} collective-permute-done((bf16[512,128]{1,0:T(8,128)(2,1)S(1)}, bf16[512,128]{1,0:T(8,128)(2,1)S(1)}, u32[]{:S(2)}, u32[]{:S(2)}) %collective-permute-start.5) | collective-permute-done | bytes 131104 | tf_op jit(solution)/shard_map/ppermute | solution.py:41
  32.5 1.9 %collective-permute-done.6 = bf16[512,128]{1,0:T(8,128)(2,1)S(1)} collective-permute-done((bf16[512,128]{1,0:T(8,128)(2,1)S(1)}, bf16[512,128]{1,0:T(8,128)(2,1)S(1)}, u32[]{:S(2)}, u32[]{:S(2)}) %collective-permute-start.6) | collective-permute-done | bytes 131104 | tf_op jit(solution)/shard_map/ppermute | solution.py:41
  34.5 0.8 maximum_bitcast_fusion.1
  36.0 25.7 %while.24 = (s32[]{:T(128)}, f32[512,1,8]{0,2,1:T(8,128)S(1)}, f32[512,1,8]{0,2,1:T(8,128)S(1)}, f32[512,1,8,128]{0,3,2,1:T(8,128)S(1)}, s32[]{:T(128)}, /*index...) while((s32[]{:T(128)}, f32[512,1,8]{0,2,1:T(8,128)S(1)}, ...), condition=%wide.region_4.5_spmd.clone, body=%wide.region_1.4_spmd.clone.sunk | while | flops 1102853120 | bytes 31992016 | solution.py:126
  36.3 2.4 %fusion.30 = (f32[512,8]{0,1:T(8,128)S(1)}, f32[512,512,8]{1,0,2:T(8,128)S(1)}) fusion(pred[512,512]{0,1:T(8,128)(4,1)S(1)} %compare_and_fusion.2, bf16[512,1,8,128]{3,0,2,1:T(8,128)(2,1)S(1)} %get-tuple-element.320, bf16[1536,1,128]{2,0,1:T(8,128)(2,1)} %get-tuple-element.319, s32[]{:T(128)S(6)} %select_n.121), kind=kOutput, calls=%fused_computation.3.clone.1 | convolution fusion | flops 543158272 | bytes 9846788 | tf_op jit(solution)/shard_map/while/body/eval_jaxpr/while/body/tkgd,nkd->tkgn/dot_general | solution.py:100
  38.7 3.7 %bitcast_add_fusion.5 = f32[512,1,8,128]{0,3,2,1:T(8,128)S(1)} fusion(f32[512,1,8,128]{0,3,2,1:T(8,128)S(1)} %get-tuple-element.302, f32[512,512,8]{1,0,2:T(8,128)S(1)} %get-tuple-element.283, f32[512,8]{0,1:T(8,128)S(1)} %bitcast.108, pred[512,512]{0,1:T(8,128)(4,1)S(1)} %compare_and_fusion.2, f32[512,8]{0,1:T(8,128)S(1)} %get-tuple-element.284, ...), kind=kOutput, calls=%fused_computation.9.clone.1 | convolution fusion | flops 548405248 | bytes 13008900 | tf_op jit(solution)/shard_map/while/body/eval_jaxpr/while/body/tkgn,nkd->tkgd/dot_general | solution.py:110
  42.4 2.0 %fusion.32 = f32[512,8]{0,1:T(8,128)S(1)} fusion(f32[512,512,8]{1,0,2:T(8,128)S(1)} %get-tuple-element.283, f32[512,8]{0,1:T(8,128)S(1)} %bitcast.109, pred[512,512]{0,1:T(8,128)(4,1)S(1)} %compare_and_fusion.2), kind=kLoop, calls=%fused_computation.5.clone.1 | loop fusion | flops 10481664 | bytes 8683520 | tf_op jit(solution)/shard_map/while/body/eval_jaxpr/while/body/reduce_sum | solution.py:109
  44.8 2.4 %fusion.30 = (f32[512,8]{0,1:T(8,128)S(1)}, f32[512,512,8]{1,0,2:T(8,128)S(1)}) fusion(pred[512,512]{0,1:T(8,128)(4,1)S(1)} %compare_and_fusion.2, bf16[512,1,8,128]{3,0,2,1:T(8,128)(2,1)S(1)} %get-tuple-element.320, bf16[1536,1,128]{2,0,1:T(8,128)(2,1)} %get-tuple-element.319, s32[]{:T(128)S(6)} %select_n.121), kind=kOutput, calls=%fused_computation.3.clone.1 | convolution fusion | flops 543158272 | bytes 9846788 | tf_op jit(solution)/shard_map/while/body/eval_jaxpr/while/body/tkgd,nkd->tkgn/dot_general | solution.py:100
  47.3 3.7 %bitcast_add_fusion.5 = f32[512,1,8,128]{0,3,2,1:T(8,128)S(1)} fusion(f32[512,1,8,128]{0,3,2,1:T(8,128)S(1)} %get-tuple-element.302, f32[512,512,8]{1,0,2:T(8,128)S(1)} %get-tuple-element.283, f32[512,8]{0,1:T(8,128)S(1)} %bitcast.108, pred[512,512]{0,1:T(8,128)(4,1)S(1)} %compare_and_fusion.2, f32[512,8]{0,1:T(8,128)S(1)} %get-tuple-element.284, ...), kind=kOutput, calls=%fused_computation.9.clone.1 | convolution fusion | flops 548405248 | bytes 13008900 | tf_op jit(solution)/shard_map/while/body/eval_jaxpr/while/body/tkgn,nkd->tkgd/dot_general | solution.py:110
  51.0 2.0 %fusion.32 = f32[512,8]{0,1:T(8,128)S(1)} fusion(f32[512,512,8]{1,0,2:T(8,128)S(1)} %get-tuple-element.283, f32[512,8]{0,1:T(8,128)S(1)} %bitcast.109, pred[512,512]{0,1:T(8,128)(4,1)S(1)} %compare_and_fusion.2), kind=kLoop, calls=%fused_computation.5.clone.1 | loop fusion | flops 10481664 | bytes 8683520 | tf_op jit(solution)/shard_map/while/body/eval_jaxpr/while/body/reduce_sum | solution.py:109
  53.4 2.4 %fusion.30 = (f32[512,8]{0,1:T(8,128)S(1)}, f32[512,512,8]{1,0,2:T(8,128)S(1)}) fusion(pred[512,512]{0,1:T(8,128)(4,1)S(1)} %compare_and_fusion.2, bf16[512,1,8,128]{3,0,2,1:T(8,128)(2,1)S(1)} %get-tuple-element.320, bf16[1536,1,128]{2,0,1:T(8,128)(2,1)} %get-tuple-element.319, s32[]{:T(128)S(6)} %select_n.121), kind=kOutput, calls=%fused_computation.3.clone.1 | convolution fusion | flops 543158272 | bytes 9846788 | tf_op jit(solution)/shard_map/while/body/eval_jaxpr/while/body/tkgd,nkd->tkgn/dot_general | solution.py:100
  55.8 3.7 %bitcast_add_fusion.5 = f32[512,1,8,128]{0,3,2,1:T(8,128)S(1)} fusion(f32[512,1,8,128]{0,3,2,1:T(8,128)S(1)} %get-tuple-element.302, f32[512,512,8]{1,0,2:T(8,128)S(1)} %get-tuple-element.283, f32[512,8]{0,1:T(8,128)S(1)} %bitcast.108, pred[512,512]{0,1:T(8,128)(4,1)S(1)} %compare_and_fusion.2, f32[512,8]{0,1:T(8,128)S(1)} %get-tuple-element.284, ...), kind=kOutput, calls=%fused_computation.9.clone.1 | convolution fusion | flops 548405248 | bytes 13008900 | tf_op jit(solution)/shard_map/while/body/eval_jaxpr/while/body/tkgn,nkd->tkgd/dot_general | solution.py:110
  59.6 2.0 %fusion.32 = f32[512,8]{0,1:T(8,128)S(1)} fusion(f32[512,512,8]{1,0,2:T(8,128)S(1)} %get-tuple-element.283, f32[512,8]{0,1:T(8,128)S(1)} %bitcast.109, pred[512,512]{0,1:T(8,128)(4,1)S(1)} %compare_and_fusion.2), kind=kLoop, calls=%fused_computation.5.clone.1 | loop fusion | flops 10481664 | bytes 8683520 | tf_op jit(solution)/shard_map/while/body/eval_jaxpr/while/body/reduce_sum | solution.py:109
  61.7 0.3 divide_convert_fusion
  62.3 0.7 copy.73
  62.9 17.1 %all_to_all.54 = bf16[4,128,1024]{2,1,0:T(8,128)(2,1)S(1)} all-to-all(bf16[4,128,1024]{2,1,0:T(8,128)(2,1)S(1)} %copy.73), channel_id=1, replica_groups=mesh['blk'=8,'uly'=4] {'uly'}, dimensions={0} | all-to-all | bytes 2097152 | tf_op jit(solution)/shard_map/all_to_all | solution.py:133
  80.1 0.7 copy.67
  80.7 1.3 %copy.68 = bf16[128,4096]{1,0:T(8,128)(2,1)} copy(bf16[128,4096]{0,1:T(8,128)(2,1)S(1)} %bitcast.112) | data formatting | bytes 2097152 | tf_op jit(solution)/shard_map/all_to_all | solution.py:133
  (36 shorter events, 2.3 us)
Async XLA Ops:
  0.0 35.9 %copy-start = (s32[512]{0:T(512)S(1)}, s32[512]{0:T(512)}, u32[]{:S(2)}) copy-start(s32[512]{0:T(512)} %param.9) | copy-start | bytes 6148
  1.1 10.4 %collective-permute-start = (bf16[1,128,128]{1,2,0:T(8,128)(2,1)S(1)}, bf16[1,128,128]{1,2,0:T(8,128)(2,1)S(1)}, u32[]{:S(2)}, u32[]{:S(2)}) collective-permute-start(bf16[1,128,128]{1,2,0:T(8,128)(2,1)S(1)} %get-tuple-element.211), channel_id=1, source_target_pairs={{0,1},{1,2},{2,3},{3,0},{4,5},{5,6},{6,7},{7,4},{8,9},{9,10},{10,1... | collective-permute-start | bytes 98312 | tf_op jit(solution)/shard_map/ppermute | solution.py:33
  1.1 16.1 %collective-permute-start.1 = (bf16[1,128,128]{1,2,0:T(8,128)(2,1)S(1)}, bf16[1,128,128]{1,2,0:T(8,128)(2,1)S(1)}, u32[]{:S(2)}, u32[]{:S(2)}) collective-permute-start(bf16[1,128,128]{1,2,0:T(8,128)(2,1)S(1)} %get-tuple-element.210), channel_id=1, source_target_pairs={{0,2},{1,3},{2,0},{3,1},{4,6},{5,7},{6,4},{7,5},{8,10},{9,11},{10,... | collective-permute-start | bytes 98312 | tf_op jit(solution)/shard_map/ppermute | solution.py:33
  2.7 14.5 %collective-permute-start.2 = (bf16[1,128,128]{1,2,0:T(8,128)(2,1)S(1)}, bf16[1,128,128]{1,2,0:T(8,128)(2,1)S(1)}, u32[]{:S(2)}, u32[]{:S(2)}) collective-permute-start(bf16[1,128,128]{1,2,0:T(8,128)(2,1)S(1)} %get-tuple-element.209), channel_id=1, source_target_pairs={{0,3},{1,0},{2,1},{3,2},{4,7},{5,4},{6,5},{7,6},{8,11},{9,8},{10,9... | collective-permute-start | bytes 98312 | tf_op jit(solution)/shard_map/ppermute | solution.py:33
  5.8 7.9 %all-to-all-start.1 = ((bf16[128,4,128]{0,2,1:T(8,128)(2,1)}), bf16[128,4,128]{0,2,1:T(8,128)(2,1)S(1)}, u32[]{:S(2)}, u32[]{:S(2)}) async-start(bf16[128,4,128]{0,2,1:T(8,128)(2,1)} %bitcast.8), calls=%async_computation.1 | async-start | bytes 262144 | tf_op jit(solution)/shard_map/all_to_all | solution.py:58
  13.7 21.6 %all-to-all-start = ((bf16[128,4,1024]{2,0,1:T(8,128)(2,1)}), bf16[128,4,1024]{2,0,1:T(8,128)(2,1)S(1)}, u32[]{:S(2)}, u32[]{:S(2)}) async-start(bf16[128,4,1024]{2,0,1:T(8,128)(2,1)} %bitcast.85), calls=%async_computation | async-start | bytes 2097152 | tf_op jit(solution)/shard_map/all_to_all | solution.py:55
  17.4 11.7 %collective-permute-start.3 = (bf16[512,128]{1,0:T(8,128)(2,1)S(1)}, bf16[512,128]{1,0:T(8,128)(2,1)S(1)}, u32[]{:S(2)}, u32[]{:S(2)}) collective-permute-start(bf16[512,128]{1,0:T(8,128)(2,1)S(1)} %bitcast.117), channel_id=1, source_target_pairs={{0,8},{4,12},{8,16},{12,20},{16,24},{20,28},{1,9},{5,13},{9,17},{1... | collective-permute-start | bytes 393224 | tf_op jit(solution)/shard_map/ppermute | solution.py:41
  20.9 8.2 %collective-permute-start.4 = (bf16[512,128]{1,0:T(8,128)(2,1)S(1)}, bf16[512,128]{1,0:T(8,128)(2,1)S(1)}, u32[]{:S(2)}, u32[]{:S(2)}) collective-permute-start(bf16[512,128]{1,0:T(8,128)(2,1)S(1)} %bitcast.118), channel_id=1, source_target_pairs={{0,4},{4,8},{8,12},{12,16},{16,20},{20,24},{24,28},{1,5},{5,9},{9,... | collective-permute-start | bytes 393224 | tf_op jit(solution)/shard_map/ppermute | solution.py:41
  25.1 7.5 %collective-permute-start.5 = (bf16[512,128]{1,0:T(8,128)(2,1)S(1)}, bf16[512,128]{1,0:T(8,128)(2,1)S(1)}, u32[]{:S(2)}, u32[]{:S(2)}) collective-permute-start(bf16[512,128]{1,0:T(8,128)(2,1)S(1)} %bitcast.120), channel_id=1, source_target_pairs={{0,8},{4,12},{8,16},{12,20},{16,24},{20,28},{1,9},{5,13},{9,17},{1... | collective-permute-start | bytes 393224 | tf_op jit(solution)/shard_map/ppermute | solution.py:41
  27.0 7.5 %collective-permute-start.6 = (bf16[512,128]{1,0:T(8,128)(2,1)S(1)}, bf16[512,128]{1,0:T(8,128)(2,1)S(1)}, u32[]{:S(2)}, u32[]{:S(2)}) collective-permute-start(bf16[512,128]{1,0:T(8,128)(2,1)S(1)} %bitcast.121), channel_id=1, source_target_pairs={{0,4},{4,8},{8,12},{12,16},{16,20},{20,24},{24,28},{1,5},{5,9},{9,... | collective-permute-start | bytes 393224 | tf_op jit(solution)/shard_map/ppermute | solution.py:41
